TPU v7x, 512 devices: a whole 4x8x8 slice. The times are simulated.
512 devices in a mesh: ctx: 64 (over z_hi, y, core), tp: 8 (over x, z_lo).
Axes of the slice: x: 4, y: 8, z: 8 (z_hi: 4, z_lo: 2; z = z_hi * 2 + z_lo), core: 2. Of those that a mesh axis runs over, the one named last changes fastest.
Arguments:
- query_in: bfloat16 [1024, 16384], P('tp', 'ctx'), may hold values from -6 to 6
- key_in: bfloat16 [1024, 16384], P('tp', 'ctx'), may hold values from -6 to 6
- value_in: bfloat16 [1024, 16384], P('tp', 'ctx'), may hold values from -6 to 6
- short_kernel: float32 [3, 1024, 7], P(None, 'tp'), may hold values from -2 to 2
- basis_weight: float32 [64, 33], replicated, may hold values from -96 to 96
- basis_bias: float32 [64], replicated, may hold values from -3.140625 to 3.140625
- filter_proj: float32 [1024, 64], P('tp'), may hold values from -0.75 to 0.75
- decay_rate: float32 [1024], P('tp'), as said below
- skip_gain: float32 [1024], P('tp'), may hold values from -3 to 3
- grad_out: bfloat16 [1024, 16384], P('tp', 'ctx'), may hold values from -6 to 6
Outputs:
- mixed: bfloat16 [1024, 16384], P('tp', 'ctx')
- grad_query: bfloat16 [1024, 16384], P('tp', 'ctx')
- grad_key: bfloat16 [1024, 16384], P('tp', 'ctx')
- grad_value: bfloat16 [1024, 16384], P('tp', 'ctx')
- grad_proj: float32 [1024, 64], P('tp')
- grad_basis: float32 [64, 33], replicated
Inputs may be any that keep to these rules, and one draw needn't show every extreme that they name: decay_rate is positive in every channel.
All inputs are finite; a program needn't handle non-finite values.
Results may differ from a plain program's by a relative error of at most 0.0066.
Values may be sent and summed in bfloat16 or wider, within the bound.
No kernel may reach another device: no remote copies, remote signals or barrier semaphores. Data moves between devices by JAX's collectives and lax.ppermute only.
A program may use at most 64 MiB of HBM per device.

v0:
```python
import math
import jax
import jax.numpy as jnp
from jax import lax
from jax.sharding import PartitionSpec as P

PRECISE = lax.Precision.HIGHEST


def passed_along(value, axis, steps):
    count = lax.axis_size(axis)
    leading, last = (max(0, -steps), min(count, count - steps))
    return lax.ppermute(value, axis, [(source, source + steps) for source in range(leading, last)])


def features(offset_pos, num_pos, seq_total, num_freq):
    positions = offset_pos + jnp.arange(num_pos, dtype=jnp.int32)
    pieces = [positions.astype(jnp.float32) / seq_total]
    for harmonic in range(1, num_freq + 1):
        angles = (harmonic * positions % seq_total).astype(jnp.float32) * (
            2.0 * math.pi / seq_total
        )
        pieces.append(jnp.cos(angles))
        pieces.append(jnp.sin(angles))
    return jnp.stack(pieces)


def window(decay_rate, offset_pos, num_pos, seq_total):
    positions = (offset_pos + jnp.arange(num_pos, dtype=jnp.int32)).astype(jnp.float32)
    energy = jnp.expm1(-2.0 * decay_rate) / jnp.expm1(-2.0 * decay_rate / seq_total)
    return (
        jnp.exp(-(decay_rate[:, None] * positions[None, :]) / seq_total) / jnp.sqrt(energy)[:, None]
    )


def featurize_rim(signal, before, kernel):
    extended = jnp.concatenate([before, signal], axis=1).astype(jnp.float32)
    num_taps = kernel.shape[1]
    rim_len = num_taps - 1
    num_tok = signal.shape[1]
    result = kernel[:, 0:1] * extended[:, rim_len:]
    for offset in range(1, num_taps):
        result = (
            result
            + kernel[:, offset : offset + 1]
            * extended[:, rim_len - offset : rim_len - offset + num_tok]
        )
    return result


def featurize_back(signal, following, kernel):
    extended = jnp.concatenate([signal, following], axis=1).astype(jnp.float32)
    num_taps = kernel.shape[1]
    num_tok = signal.shape[1]
    result = kernel[:, 0:1] * extended[:, :num_tok]
    for offset in range(1, num_taps):
        result = result + kernel[:, offset : offset + 1] * extended[:, offset : offset + num_tok]
    return result


def tables(num_rows, num_cols, modulus):
    row_ids = jnp.arange(num_rows, dtype=jnp.int32)[:, None]
    col_ids = jnp.arange(num_cols, dtype=jnp.int32)[None, :]
    angles = (row_ids * col_ids % modulus).astype(jnp.float32) * (-2.0 * math.pi / modulus)
    return (jnp.cos(angles), jnp.sin(angles))


def spectrum(signal, outer, twiddle, inner):
    num_chan = signal.shape[0]
    folded = signal.reshape(num_chan, outer[0].shape[1], inner[0].shape[0])
    section_re = jnp.einsum("kt,nts->nks", outer[0], folded, precision=PRECISE)
    section_im = jnp.einsum("kt,nts->nks", outer[1], folded, precision=PRECISE)
    turned_re = section_re * twiddle[0] - section_im * twiddle[1]
    turned_im = section_re * twiddle[1] + section_im * twiddle[0]
    spec_re = jnp.einsum("nks,sj->nkj", turned_re, inner[0], precision=PRECISE) - jnp.einsum(
        "nks,sj->nkj", turned_im, inner[1], precision=PRECISE
    )
    spec_im = jnp.einsum("nks,sj->nkj", turned_re, inner[1], precision=PRECISE) + jnp.einsum(
        "nks,sj->nkj", turned_im, inner[0], precision=PRECISE
    )
    return (spec_re, spec_im)


def restore(spec_re, spec_im, outer, twiddle, inner):
    num_chan = spec_re.shape[0]
    padded_len = outer[0].shape[0] * inner[0].shape[0]
    back_re = jnp.einsum("nkj,sj->nks", spec_re, inner[0], precision=PRECISE) + jnp.einsum(
        "nkj,sj->nks", spec_im, inner[1], precision=PRECISE
    )
    back_im = jnp.einsum("nkj,sj->nks", spec_im, inner[0], precision=PRECISE) - jnp.einsum(
        "nkj,sj->nks", spec_re, inner[1], precision=PRECISE
    )
    turned_re = back_re * twiddle[0] + back_im * twiddle[1]
    turned_im = back_im * twiddle[0] - back_re * twiddle[1]
    result = jnp.einsum("kt,nks->nts", outer[0], turned_re, precision=PRECISE) + jnp.einsum(
        "kt,nks->nts", outer[1], turned_im, precision=PRECISE
    )
    return result.reshape(num_chan, -1) * (1.0 / padded_len)


def convolve_forward(carried_chan, filter_chan, own_skip, transform_tables):
    outer, twiddle, inner = transform_tables
    carried_wide = carried_chan.astype(jnp.float32)
    carried_re, carried_im = spectrum(carried_wide, outer, twiddle, inner)
    filter_re, filter_im = spectrum(filter_chan.astype(jnp.float32), outer, twiddle, inner)
    conv_chan = restore(
        filter_re * carried_re - filter_im * carried_im,
        filter_re * carried_im + filter_im * carried_re,
        outer,
        twiddle,
        inner,
    )
    long_chan = (conv_chan + own_skip[:, None] * carried_wide).astype(jnp.bfloat16)
    return (long_chan, (carried_re, carried_im, filter_re, filter_im))


def convolve_backward(grad_chan, spectra, own_skip, transform_tables):
    outer, twiddle, inner = transform_tables
    carried_re, carried_im, filter_re, filter_im = spectra
    grad_chan_wide = grad_chan.astype(jnp.float32)
    grad_re, grad_im = spectrum(grad_chan_wide, outer, twiddle, inner)
    carried_grad_chan = (
        restore(
            filter_re * grad_re + filter_im * grad_im,
            filter_re * grad_im - filter_im * grad_re,
            outer,
            twiddle,
            inner,
        )
        + own_skip[:, None] * grad_chan_wide
    ).astype(jnp.bfloat16)
    filter_grad_chan = restore(
        carried_re * grad_re + carried_im * grad_im,
        carried_re * grad_im - carried_im * grad_re,
        outer,
        twiddle,
        inner,
    ).astype(jnp.bfloat16)
    return (carried_grad_chan, filter_grad_chan)


def on_device(
    query_in,
    key_in,
    value_in,
    short_kernel,
    basis_weight,
    basis_bias,
    filter_proj,
    decay_rate,
    skip_gain,
    grad_out,
):
    ctx_size = lax.axis_size("ctx")
    ctx_rank = lax.axis_index("ctx")
    tp_size = lax.axis_size("tp")
    num_tok = query_in.shape[1]
    chan_local = query_in.shape[0]
    seq_total = num_tok * ctx_size
    all_channels = chan_local * tp_size
    num_freq = (basis_weight.shape[1] - 1) // 2
    feat_width = basis_weight.shape[0]
    rim_len = short_kernel.shape[2] - 1
    tok_start = ctx_rank * num_tok
    rim_edge = num_tok - rim_len
    per_dev = chan_local // ctx_size
    chan_start = ctx_rank * per_dev
    own_skip = lax.dynamic_slice_in_dim(skip_gain, chan_start, per_dev)
    proj_scale = 1.0 / math.sqrt(seq_total)
    basis_scale = math.sqrt(feat_width / (seq_total * all_channels))
    before = passed_along(
        (query_in[:, rim_edge:], key_in[:, rim_edge:], value_in[:, rim_edge:]), "ctx", 1
    )
    query_feat = featurize_rim(query_in, before[0], short_kernel[0])
    key_feat = featurize_rim(key_in, before[1], short_kernel[1])
    value_feat = featurize_rim(value_in, before[2], short_kernel[2])
    carried = (key_feat * value_feat).astype(jnp.bfloat16)
    grad_wide = grad_out.astype(jnp.float32)
    grad_long = (grad_wide * query_feat).astype(jnp.bfloat16)
    basis_rows = features(tok_start, num_tok, seq_total, num_freq)
    hidden_in = (
        jnp.dot(basis_weight, basis_rows, precision=PRECISE, preferred_element_type=jnp.float32)
        + basis_bias[:, None]
    )
    activation = jnp.sin(hidden_in)
    envelope = window(decay_rate, tok_start, num_tok, seq_total)
    filter_tok = (
        jnp.dot(filter_proj, activation, precision=PRECISE, preferred_element_type=jnp.float32)
        * envelope
    ).astype(jnp.bfloat16)
    inner_len = 2 * ctx_size
    transform_tables = (
        tables(num_tok, num_tok // 2, num_tok),
        tables(num_tok, inner_len, 2 * seq_total),
        tables(inner_len, inner_len, inner_len),
    )
    spread = (
        lax.all_to_all(carried, "ctx", split_axis=0, concat_axis=1, tiled=True),
        lax.all_to_all(filter_tok, "ctx", split_axis=0, concat_axis=1, tiled=True),
    )
    carried_chan = spread[0]
    filter_chan = spread[1]
    long_chan, spectra = convolve_forward(carried_chan, filter_chan, own_skip, transform_tables)
    long_tok = lax.all_to_all(long_chan, "ctx", split_axis=1, concat_axis=0, tiled=True)
    grad_chan = lax.all_to_all(grad_long, "ctx", split_axis=0, concat_axis=1, tiled=True)
    carried_grad_chan, filter_grad_chan = convolve_backward(
        grad_chan, spectra, own_skip, transform_tables
    )
    returned = (
        lax.all_to_all(carried_grad_chan, "ctx", split_axis=1, concat_axis=0, tiled=True),
        lax.all_to_all(filter_grad_chan, "ctx", split_axis=1, concat_axis=0, tiled=True),
    )
    carried_grad = returned[0]
    filter_grad_tok = returned[1]
    long_wide = long_tok.astype(jnp.float32)
    mixed = (query_feat * long_wide).astype(jnp.bfloat16)
    grad_query_feat = (grad_wide * long_wide).astype(jnp.bfloat16)
    grad_raw = filter_grad_tok.astype(jnp.float32) * envelope
    part_proj = jnp.dot(
        grad_raw, activation.T, precision=PRECISE, preferred_element_type=jnp.float32
    )
    grad_hidden = jnp.dot(
        filter_proj.T, grad_raw, precision=PRECISE, preferred_element_type=jnp.float32
    ) * jnp.cos(hidden_in)
    part_basis = jnp.dot(
        grad_hidden, basis_rows.T, precision=PRECISE, preferred_element_type=jnp.float32
    )
    grad_proj = lax.psum(part_proj, "ctx") * proj_scale
    grad_basis = lax.psum(part_basis, ("ctx", "tp")) * basis_scale
    carried_grad_wide = carried_grad.astype(jnp.float32)
    grad_key_feat = (carried_grad_wide * value_feat).astype(jnp.bfloat16)
    grad_value_feat = (carried_grad_wide * key_feat).astype(jnp.bfloat16)
    following = passed_along(
        (grad_query_feat[:, :rim_len], grad_key_feat[:, :rim_len], grad_value_feat[:, :rim_len]),
        "ctx",
        -1,
    )
    grad_query = featurize_back(grad_query_feat, following[0], short_kernel[0]).astype(jnp.bfloat16)
    grad_key = featurize_back(grad_key_feat, following[1], short_kernel[1]).astype(jnp.bfloat16)
    grad_value = featurize_back(grad_value_feat, following[2], short_kernel[2]).astype(jnp.bfloat16)
    return (mixed, grad_query, grad_key, grad_value, grad_proj, grad_basis)


def solution(mesh):
    return jax.shard_map(
        on_device,
        mesh=mesh,
        in_specs=(
            P("tp", "ctx"),
            P("tp", "ctx"),
            P("tp", "ctx"),
            P(None, "tp", None),
            P(),
            P(),
            P("tp", None),
            P("tp"),
            P("tp"),
            P("tp", "ctx"),
        ),
        out_specs=(
            P("tp", "ctx"),
            P("tp", "ctx"),
            P("tp", "ctx"),
            P("tp", "ctx"),
            P("tp", None),
            P(),
        ),
        check_vma=False,
    )
```

profile of v0, /device:TPU:1, one launch (start us, length us, event | category | flops | bytes accessed | tf_op | source)
XLA Modules:
  0.0 538.5 jit_solution(8369667688324918726)
XLA Ops:
  0.6 0.8 slice.242
  1.5 4.6 collective-permute-start
  7.5 0.6 copy-done.9
  9.7 0.7 all_to_all.60
  10.4 15.5 %all-to-all-start = ((bf16[64,2,256]{2,1,0:T(2,128)(2,1)}), bf16[64,2,256]{2,1,0:T(2,128)(2,1)S(1)}, u32[]{:S(2)}, u32[]{:S(2)}) async-start(bf16[64,2,256]{2,1,0:T(2,128)(2,1)} %all_to_all.60), calls=%async_computation | async-start | bytes 131072 | tf_op jit(solution)/shard_map/all_to_all | solution.py:199
  26.0 3.5 collective-permute-start.2
  29.6 2.2 collective-permute-start.1
  33.1 0.6 copy-done.8
  33.9 0.7 copy-done.1
  35.1 0.7 all_to_all.67
  35.7 2.4 all-to-all-done
  38.1 9.7 %all-to-all-start.3 = ((bf16[64,2,256]{2,1,0:T(2,128)(2,1)}), bf16[64,2,256]{2,1,0:T(2,128)(2,1)S(1)}, u32[]{:S(2)}, u32[]{:S(2)}) async-start(bf16[64,2,256]{2,1,0:T(2,128)(2,1)} %all_to_all.67), calls=%async_computation.3 | async-start | bytes 131072 | tf_op jit(solution)/shard_map/all_to_all | solution.py:205
  47.8 0.8 convolution_bitcast_fusion.4
  48.6 0.8 convolution_bitcast_fusion.5
  49.4 0.8 fusion.144
  50.1 0.8 convolution_subtract_fusion.5
  50.9 0.8 fusion.121
  51.7 7.9 %all-to-all-done.3 = bf16[64,2,256]{2,1,0:T(2,128)(2,1)S(1)} async-done(((bf16[64,2,256]{2,1,0:T(2,128)(2,1)}), bf16[64,2,256]{2,1,0:T(2,128)(2,1)S(1)}, u32[]{:S(2)}, u32[]{:S(2)}) %all-to-all-start.3) | async-done | bytes 65568 | tf_op jit(solution)/shard_map/all_to_all | solution.py:205
  59.6 0.8 convolution_bitcast_fusion
  60.4 0.8 convolution_bitcast_fusion.1
  61.2 0.8 fusion.134
  62.0 0.8 fusion.114
  62.7 0.8 convolution_subtract_fusion.2
  63.5 0.8 convolution_add_fusion.2
  64.3 0.8 multiply_add_fusion.1
  66.3 0.6 convolution_add_fusion.1
  66.9 0.6 convolution_subtract_fusion.1
  67.6 11.5 %fusion.19 = f32[2,128,128]{2,1,0:T(8,128)S(1)} fusion(f32[2,256,128]{1,2,0:T(8,128)S(1)} %convolution_subtract_fusion.1, f32[2,256,128]{1,2,0:T(8,128)S(1)} %convolution_add_fusion.1, f32[256,128]{0,1:T(8,128)S(1)} %copy.206, f32[256,128]{0,1:T(8,128)S(1)} %copy.204), kind=kOutput, calls=%fused_computation.45 | convolution fusion | flops 101318656 | bytes 917504 | tf_op jit(solution)/shard_map/kt,nks->nts/dot_general | solution.py:95
  79.1 0.9 fusion.2
  80.2 0.7 copy.236
  80.9 4.8 all-to-all-start.4
  86.0 12.0 %all-to-all-done.4 = bf16[2,64,256]{2,0,1:T(2,128)(2,1)S(1)} async-done(((bf16[2,64,256]{2,0,1:T(2,128)(2,1)}), bf16[2,64,256]{2,0,1:T(2,128)(2,1)S(1)}, u32[]{:S(2)}, u32[]{:S(2)}) %all-to-all-start.4) | async-done | bytes 65568 | tf_op jit(solution)/shard_map/all_to_all | solution.py:210
  98.5 2.3 collective-permute-start.5
  101.3 0.7 all_to_all.63
  101.9 6.0 %all-to-all-start.1 = ((bf16[64,2,256]{2,1,0:T(2,128)(2,1)}), bf16[64,2,256]{2,1,0:T(2,128)(2,1)S(1)}, u32[]{:S(2)}, u32[]{:S(2)}) async-start(bf16[64,2,256]{2,1,0:T(2,128)(2,1)} %all_to_all.63), calls=%async_computation.1 | async-start | bytes 131072 | tf_op jit(solution)/shard_map/all_to_all | solution.py:198
  108.0 2.4 collective-permute-start.4
  110.4 1.0 fusion.37
  111.4 2.1 collective-permute-done.4
  113.5 1.0 fusion.44
  114.5 5.6 %all-to-all-done.1 = bf16[64,2,256]{2,1,0:T(2,128)(2,1)S(1)} async-done(((bf16[64,2,256]{2,1,0:T(2,128)(2,1)}), bf16[64,2,256]{2,1,0:T(2,128)(2,1)S(1)}, u32[]{:S(2)}, u32[]{:S(2)}) %all-to-all-start.1) | async-done | bytes 65568 | tf_op jit(solution)/shard_map/all_to_all | solution.py:198
  120.2 0.8 convolution_bitcast_fusion.2
  121.0 0.8 convolution_bitcast_fusion.3
  121.8 0.8 fusion.119
  122.5 0.8 fusion.142
  123.3 0.8 convolution_subtract_fusion.4
  124.0 0.8 multiply_add_fusion
  126.1 0.6 convolution_add_fusion
  126.8 0.6 convolution_subtract_fusion
  127.4 0.9 fusion.12
  128.3 0.9 fusion.8
  129.3 0.7 copy.242
  130.0 7.0 %all-to-all-start.5 = ((bf16[2,64,256]{2,0,1:T(2,128)(2,1)}), bf16[2,64,256]{2,0,1:T(2,128)(2,1)S(1)}, u32[]{:S(2)}, u32[]{:S(2)}) async-start(bf16[2,64,256]{2,0,1:T(2,128)(2,1)} %copy.242), calls=%async_computation.5 | async-start | bytes 131072 | tf_op jit(solution)/shard_map/all_to_all | solution.py:211
  138.3 0.6 convolution_add_fusion.3
  138.9 0.6 convolution_subtract_fusion.3
  139.6 0.9 fusion.26
  140.5 0.9 fusion.4
  141.6 0.7 copy.223
  142.3 6.9 %all-to-all-done.5 = bf16[2,64,256]{2,0,1:T(2,128)(2,1)S(1)} async-done(((bf16[2,64,256]{2,0,1:T(2,128)(2,1)}), bf16[2,64,256]{2,0,1:T(2,128)(2,1)S(1)}, u32[]{:S(2)}, u32[]{:S(2)}) %all-to-all-start.5) | async-done | bytes 65568 | tf_op jit(solution)/shard_map/all_to_all | solution.py:211
  149.2 5.8 %all-to-all-start.2 = ((bf16[2,64,256]{2,0,1:T(2,128)(2,1)}), bf16[2,64,256]{2,0,1:T(2,128)(2,1)S(1)}, u32[]{:S(2)}, u32[]{:S(2)}) async-start(bf16[2,64,256]{2,0,1:T(2,128)(2,1)} %copy.223), calls=%async_computation.2 | async-start | bytes 131072 | tf_op jit(solution)/shard_map/all_to_all | solution.py:204
  156.2 99.6 %psum.15 = f32[64,33]{0,1:T(8,128)S(1)} all-reduce(f32[64,33]{0,1:T(8,128)S(1)} %fusion.423), channel_id=1, replica_groups=mesh['ctx'=64,'tp'=8] {'ctx','tp'}, use_global_device_ids=true, to_apply=%region_1.2 | all-reduce | flops 2112 | bytes 16896 | tf_op jit(solution)/shard_map/psum | solution.py:229
  255.8 270.7 %psum.14 = f32[128,64]{0,1:T(8,128)S(1)} all-reduce(f32[128,64]{0,1:T(8,128)S(1)} %fusion.417), channel_id=1, replica_groups=mesh['ctx'=64,'tp'=8] {'ctx'}, use_global_device_ids=true, to_apply=%region_0.1 | all-reduce | flops 8192 | bytes 65536 | tf_op jit(solution)/shard_map/psum | solution.py:228
  527.3 0.7 fusion.30
  528.0 8.4 %collective-permute-start.3 = (bf16[128,6]{1,0:T(8,128)(2,1)S(1)}, bf16[128,6]{1,0:T(8,128)(2,1)S(1)}, u32[]{:S(2)}, u32[]{:S(2)}) collective-permute-start(bf16[128,6]{1,0:T(8,128)(2,1)S(1)} %slice.333), channel_id=1, source_target_pairs={{8,0},{16,8},{24,16},{32,24},{40,32},{48,40},{56,48},{64,56},{72,6... | collective-permute-start | bytes 4616 | tf_op jit(solution)/shard_map/ppermute | solution.py:13
  537.3 1.0 fusion.51
  (100 shorter events, 13.3 us)
Async XLA Ops:
  0.6 8.8 %copy-start = (f32[128,64]{0,1:T(8,128)S(1)}, f32[128,64]{0,1:T(8,128)}, u32[]{:S(2)}) copy-start(f32[128,64]{0,1:T(8,128)} %param.16) | copy-start | bytes 98308
  1.5 32.3 %collective-permute-start = (bf16[128,6]{1,0:T(8,128)(2,1)S(1)}, bf16[128,6]{1,0:T(8,128)(2,1)S(1)}, u32[]{:S(2)}, u32[]{:S(2)}) collective-permute-start(bf16[128,6]{1,0:T(8,128)(2,1)S(1)} %slice.242), channel_id=1, source_target_pairs={{0,8},{8,16},{16,24},{24,32},{32,40},{40,48},{48,56},{56,64},{64,7... | collective-permute-start | bytes 4616 | tf_op jit(solution)/shard_map/ppermute | solution.py:13
  7.5 0.7 copy-start.9
  8.2 0.7 copy-start.5
  8.2 0.7 copy-start.7
  10.4 15.5 %copy-start.3 = (bf16[128,256]{1,0:T(8,128)(2,1)S(1)}, bf16[128,256]{1,0:T(8,128)(2,1)}, u32[]{:S(2)}) copy-start(bf16[128,256]{1,0:T(8,128)(2,1)} %param.12) | copy-start | bytes 196612
  10.4 27.7 %all-to-all-start = ((bf16[64,2,256]{2,1,0:T(2,128)(2,1)}), bf16[64,2,256]{2,1,0:T(2,128)(2,1)S(1)}, u32[]{:S(2)}, u32[]{:S(2)}) async-start(bf16[64,2,256]{2,1,0:T(2,128)(2,1)} %all_to_all.60), calls=%async_computation | async-start | bytes 131072 | tf_op jit(solution)/shard_map/all_to_all | solution.py:199
  25.9 3.6 copy-start.4
  26.0 59.8 %collective-permute-start.2 = (bf16[128,6]{1,0:T(8,128)(2,1)S(1)}, bf16[128,6]{1,0:T(8,128)(2,1)S(1)}, u32[]{:S(2)}, u32[]{:S(2)}) collective-permute-start(bf16[128,6]{1,0:T(8,128)(2,1)S(1)} %slice.274), channel_id=1, source_target_pairs={{0,8},{8,16},{16,24},{24,32},{32,40},{40,48},{48,56},{56,64},{64,7... | collective-permute-start | bytes 4616 | tf_op jit(solution)/shard_map/ppermute | solution.py:13
  29.6 2.7 copy-start.6
  29.6 56.3 %collective-permute-start.1 = (bf16[128,6]{1,0:T(8,128)(2,1)S(1)}, bf16[128,6]{1,0:T(8,128)(2,1)S(1)}, u32[]{:S(2)}, u32[]{:S(2)}) collective-permute-start(bf16[128,6]{1,0:T(8,128)(2,1)S(1)} %slice.258), channel_id=1, source_target_pairs={{0,8},{8,16},{16,24},{24,32},{32,40},{40,48},{48,56},{56,64},{64,7... | collective-permute-start | bytes 4616 | tf_op jit(solution)/shard_map/ppermute | solution.py:13
  33.0 0.9 copy-start.2
  33.1 0.7 copy-start.8
  33.8 0.8 copy-start.1
  38.1 21.5 %all-to-all-start.3 = ((bf16[64,2,256]{2,1,0:T(2,128)(2,1)}), bf16[64,2,256]{2,1,0:T(2,128)(2,1)S(1)}, u32[]{:S(2)}, u32[]{:S(2)}) async-start(bf16[64,2,256]{2,1,0:T(2,128)(2,1)} %all_to_all.67), calls=%async_computation.3 | async-start | bytes 131072 | tf_op jit(solution)/shard_map/all_to_all | solution.py:205
  80.9 17.0 %all-to-all-start.4 = ((bf16[2,64,256]{2,0,1:T(2,128)(2,1)}), bf16[2,64,256]{2,0,1:T(2,128)(2,1)S(1)}, u32[]{:S(2)}, u32[]{:S(2)}) async-start(bf16[2,64,256]{2,0,1:T(2,128)(2,1)} %copy.236), calls=%async_computation.4 | async-start | bytes 131072 | tf_op jit(solution)/shard_map/all_to_all | solution.py:210
  98.5 11.8 %collective-permute-start.5 = (bf16[128,6]{1,0:T(8,128)(2,1)S(1)}, bf16[128,6]{1,0:T(8,128)(2,1)S(1)}, u32[]{:S(2)}, u32[]{:S(2)}) collective-permute-start(bf16[128,6]{1,0:T(8,128)(2,1)S(1)} %slice.349), channel_id=1, source_target_pairs={{8,0},{16,8},{24,16},{32,24},{40,32},{48,40},{56,48},{64,56},{72,6... | collective-permute-start | bytes 4616 | tf_op jit(solution)/shard_map/ppermute | solution.py:13
  101.9 18.2 %all-to-all-start.1 = ((bf16[64,2,256]{2,1,0:T(2,128)(2,1)}), bf16[64,2,256]{2,1,0:T(2,128)(2,1)S(1)}, u32[]{:S(2)}, u32[]{:S(2)}) async-start(bf16[64,2,256]{2,1,0:T(2,128)(2,1)} %all_to_all.63), calls=%async_computation.1 | async-start | bytes 131072 | tf_op jit(solution)/shard_map/all_to_all | solution.py:198
  108.0 5.5 %collective-permute-start.4 = (bf16[128,6]{1,0:T(8,128)(2,1)S(1)}, bf16[128,6]{1,0:T(8,128)(2,1)S(1)}, u32[]{:S(2)}, u32[]{:S(2)}) collective-permute-start(bf16[128,6]{1,0:T(8,128)(2,1)S(1)} %slice.341), channel_id=1, source_target_pairs={{8,0},{16,8},{24,16},{32,24},{40,32},{48,40},{56,48},{64,56},{72,6... | collective-permute-start | bytes 4616 | tf_op jit(solution)/shard_map/ppermute | solution.py:13
  130.0 19.1 %all-to-all-start.5 = ((bf16[2,64,256]{2,0,1:T(2,128)(2,1)}), bf16[2,64,256]{2,0,1:T(2,128)(2,1)S(1)}, u32[]{:S(2)}, u32[]{:S(2)}) async-start(bf16[2,64,256]{2,0,1:T(2,128)(2,1)} %copy.242), calls=%async_computation.5 | async-start | bytes 131072 | tf_op jit(solution)/shard_map/all_to_all | solution.py:211
  149.2 378.0 %all-to-all-start.2 = ((bf16[2,64,256]{2,0,1:T(2,128)(2,1)}), bf16[2,64,256]{2,0,1:T(2,128)(2,1)S(1)}, u32[]{:S(2)}, u32[]{:S(2)}) async-start(bf16[2,64,256]{2,0,1:T(2,128)(2,1)} %copy.223), calls=%async_computation.2 | async-start | bytes 131072 | tf_op jit(solution)/shard_map/all_to_all | solution.py:204
  528.0 9.3 %collective-permute-start.3 = (bf16[128,6]{1,0:T(8,128)(2,1)S(1)}, bf16[128,6]{1,0:T(8,128)(2,1)S(1)}, u32[]{:S(2)}, u32[]{:S(2)}) collective-permute-start(bf16[128,6]{1,0:T(8,128)(2,1)S(1)} %slice.333), channel_id=1, source_target_pairs={{8,0},{16,8},{24,16},{32,24},{40,32},{48,40},{56,48},{64,56},{72,6... | collective-permute-start | bytes 4616 | tf_op jit(solution)/shard_map/ppermute | solution.py:13
where the time goes:
time: 544 us; the launch traced here: 539 us
  blocking collectives  370 us (68%)
  starting transfers between devices  72.2 us (13%)
  matrix products  39.1 us (7%)
  waiting for transfers between devices  37.1 us (7%)
  other arithmetic  9.16 us (2%)
  local copies, waits for them, and re-layouts  8.96 us (2%)
    psum x1, blocking collectives, on_device(): grad_proj = lax.psum(part_proj, 'ctx') * proj_scale  271 us
    psum x1, blocking collectives, on_device(): grad_basis = lax.psum(part_basis, ('ctx', 'tp')) * basis_scale  99.6 us
    ppermute x6, starting transfers between devices, passed_along(): lax.ppermute(value, axis, [(source, source + steps) for source in range(l...  23.4 us
    all_to_all x1, starting transfers between devices, on_device(): lax.all_to_all(filter_tok, 'ctx', split_axis=0, concat_axis=1, tiled=True)  15.5 us
    dot_general x3, matrix products, restore(): jnp.einsum('kt,nks->nts', outer[0], turned_re, precision=PRECISE)  13.3 us
    all_to_all x1, waiting for transfers between devices, on_device(): lax.all_to_all(carried_grad_chan, 'ctx', split_axis=1, concat_axis=0, til...  12 us
  transfers between devices with their start and end apart: 12, of which 7 were waited for; matrix products, arithmetic and copies ran while one was open for 7% of the time, Pallas kernels for 0%

commit v1 on v0

--- a/solution.py
+++ b/solution.py
@@ -5,6 +5,11 @@
 from jax.sharding import PartitionSpec as P
 
 PRECISE = lax.Precision.HIGHEST
+
+
+def axis_by_axis(x, one, other):
+    half = lax.psum(x, one)
+    return lax.psum(half, other)
 
 
 def passed_along(value, axis, steps):
@@ -226,7 +231,7 @@
         grad_hidden, basis_rows.T, precision=PRECISE, preferred_element_type=jnp.float32
     )
     grad_proj = lax.psum(part_proj, "ctx") * proj_scale
-    grad_basis = lax.psum(part_basis, ("ctx", "tp")) * basis_scale
+    grad_basis = axis_by_axis(part_basis, "ctx", "tp") * basis_scale
     carried_grad_wide = carried_grad.astype(jnp.float32)
     grad_key_feat = (carried_grad_wide * value_feat).astype(jnp.bfloat16)
     grad_value_feat = (carried_grad_wide * key_feat).astype(jnp.bfloat16)

time: 544 us -> 484 us (0.89)
  blocking collectives: 370 us -> 303 us
  starting transfers between devices: 72.2 us -> 79.2 us
    psum x1, blocking collectives: 99.6 us -> 27.4 us  [axis_by_axis(): return lax.psum(half, other)]
    ppermute x6, starting transfers between devices: 23.4 us -> 30.4 us  [passed_along(): lax.ppermute(value, axis, [(source, source + steps) for source in range(l...]
  transfers between devices with their start and end apart: 12 -> 12, of which waited for: 7 -> 7; matrix products, arithmetic and copies ran while one was open for 7% -> 8% of each run, Pallas kernels for 0% -> 0%
where the time goes in v1:
time: 484 us; the launch traced here: 478 us
  blocking collectives  303 us (63%)
  starting transfers between devices  79.2 us (16%)
  matrix products  39.1 us (8%)
  waiting for transfers between devices  37.1 us (8%)
  other arithmetic  9.16 us (2%)
  local copies, waits for them, and re-layouts  8.96 us (2%)
    psum x1, blocking collectives, on_device(): grad_proj = lax.psum(part_proj, 'ctx') * proj_scale  276 us
    ppermute x6, starting transfers between devices, passed_along(): lax.ppermute(value, axis, [(source, source + steps) for source in range(l...  30.4 us
    psum x1, blocking collectives, axis_by_axis(): return lax.psum(half, other)  27.4 us
    all_to_all x1, starting transfers between devices, on_device(): lax.all_to_all(filter_tok, 'ctx', split_axis=0, concat_axis=1, tiled=True)  15.5 us
    dot_general x3, matrix products, restore(): jnp.einsum('kt,nks->nts', outer[0], turned_re, precision=PRECISE)  13.3 us
    all_to_all x1, waiting for transfers between devices, on_device(): lax.all_to_all(carried_grad_chan, 'ctx', split_axis=1, concat_axis=0, til...  12 us
  transfers between devices with their start and end apart: 12, of which 7 were waited for; matrix products, arithmetic and copies ran while one was open for 8% of the time, Pallas kernels for 0%

profile of v1, /device:TPU:1, one launch (start us, length us, event | category | flops | bytes accessed | tf_op | source)
XLA Modules:
  0.0 478.1 jit_solution(12756111540021453274)
XLA Ops:
  0.6 0.8 slice.242
  1.5 4.6 collective-permute-start
  7.5 0.6 copy-done.9
  9.7 0.7 all_to_all.60
  10.4 15.5 %all-to-all-start = ((bf16[64,2,256]{2,1,0:T(2,128)(2,1)}), bf16[64,2,256]{2,1,0:T(2,128)(2,1)S(1)}, u32[]{:S(2)}, u32[]{:S(2)}) async-start(bf16[64,2,256]{2,1,0:T(2,128)(2,1)} %all_to_all.60), calls=%async_computation | async-start | bytes 131072 | tf_op jit(solution)/shard_map/all_to_all | solution.py:204
  26.0 3.5 collective-permute-start.2
  29.6 2.2 collective-permute-start.1
  33.1 0.6 copy-done.8
  33.9 0.7 copy-done.1
  35.1 0.7 all_to_all.67
  35.7 2.4 all-to-all-done
  38.1 9.7 %all-to-all-start.3 = ((bf16[64,2,256]{2,1,0:T(2,128)(2,1)}), bf16[64,2,256]{2,1,0:T(2,128)(2,1)S(1)}, u32[]{:S(2)}, u32[]{:S(2)}) async-start(bf16[64,2,256]{2,1,0:T(2,128)(2,1)} %all_to_all.67), calls=%async_computation.3 | async-start | bytes 131072 | tf_op jit(solution)/shard_map/all_to_all | solution.py:210
  47.8 0.8 convolution_bitcast_fusion.4
  48.6 0.8 convolution_bitcast_fusion.5
  49.4 0.8 fusion.144
  50.1 0.8 convolution_subtract_fusion.5
  50.9 0.8 fusion.121
  51.7 7.9 %all-to-all-done.3 = bf16[64,2,256]{2,1,0:T(2,128)(2,1)S(1)} async-done(((bf16[64,2,256]{2,1,0:T(2,128)(2,1)}), bf16[64,2,256]{2,1,0:T(2,128)(2,1)S(1)}, u32[]{:S(2)}, u32[]{:S(2)}) %all-to-all-start.3) | async-done | bytes 65568 | tf_op jit(solution)/shard_map/all_to_all | solution.py:210
  59.6 0.8 convolution_bitcast_fusion
  60.4 0.8 convolution_bitcast_fusion.1
  61.2 0.8 fusion.134
  62.0 0.8 fusion.114
  62.7 0.8 convolution_subtract_fusion.2
  63.5 0.8 convolution_add_fusion.2
  64.3 0.8 multiply_add_fusion.1
  66.3 0.6 convolution_add_fusion.1
  66.9 0.6 convolution_subtract_fusion.1
  67.6 11.5 %fusion.19 = f32[2,128,128]{2,1,0:T(8,128)S(1)} fusion(f32[2,256,128]{1,2,0:T(8,128)S(1)} %convolution_subtract_fusion.1, f32[2,256,128]{1,2,0:T(8,128)S(1)} %convolution_add_fusion.1, f32[256,128]{0,1:T(8,128)S(1)} %copy.206, f32[256,128]{0,1:T(8,128)S(1)} %copy.204), kind=kOutput, calls=%fused_computation.45 | convolution fusion | flops 101318656 | bytes 917504 | tf_op jit(solution)/shard_map/kt,nks->nts/dot_general | solution.py:100
  79.1 0.9 fusion.2
  80.2 0.7 copy.236
  80.9 4.8 %all-to-all-start.4 = ((bf16[2,64,256]{2,0,1:T(2,128)(2,1)}), bf16[2,64,256]{2,0,1:T(2,128)(2,1)S(1)}, u32[]{:S(2)}, u32[]{:S(2)}) async-start(bf16[2,64,256]{2,0,1:T(2,128)(2,1)} %copy.236), calls=%async_computation.4 | async-start | bytes 131072 | tf_op jit(solution)/shard_map/all_to_all | solution.py:215
  86.0 12.0 %all-to-all-done.4 = bf16[2,64,256]{2,0,1:T(2,128)(2,1)S(1)} async-done(((bf16[2,64,256]{2,0,1:T(2,128)(2,1)}), bf16[2,64,256]{2,0,1:T(2,128)(2,1)S(1)}, u32[]{:S(2)}, u32[]{:S(2)}) %all-to-all-start.4) | async-done | bytes 65568 | tf_op jit(solution)/shard_map/all_to_all | solution.py:215
  98.5 2.3 collective-permute-start.5
  101.3 0.7 all_to_all.63
  101.9 6.0 %all-to-all-start.1 = ((bf16[64,2,256]{2,1,0:T(2,128)(2,1)}), bf16[64,2,256]{2,1,0:T(2,128)(2,1)S(1)}, u32[]{:S(2)}, u32[]{:S(2)}) async-start(bf16[64,2,256]{2,1,0:T(2,128)(2,1)} %all_to_all.63), calls=%async_computation.1 | async-start | bytes 131072 | tf_op jit(solution)/shard_map/all_to_all | solution.py:203
  108.0 2.4 collective-permute-start.4
  110.4 1.0 fusion.37
  111.4 2.1 collective-permute-done.4
  113.5 1.0 fusion.44
  114.5 5.6 %all-to-all-done.1 = bf16[64,2,256]{2,1,0:T(2,128)(2,1)S(1)} async-done(((bf16[64,2,256]{2,1,0:T(2,128)(2,1)}), bf16[64,2,256]{2,1,0:T(2,128)(2,1)S(1)}, u32[]{:S(2)}, u32[]{:S(2)}) %all-to-all-start.1) | async-done | bytes 65568 | tf_op jit(solution)/shard_map/all_to_all | solution.py:203
  120.2 0.8 convolution_bitcast_fusion.2
  121.0 0.8 convolution_bitcast_fusion.3
  121.8 0.8 fusion.119
  122.5 0.8 fusion.142
  123.3 0.8 convolution_subtract_fusion.4
  124.0 0.8 multiply_add_fusion
  126.1 0.6 convolution_add_fusion
  126.8 0.6 convolution_subtract_fusion
  127.4 0.9 fusion.12
  128.3 0.9 fusion.8
  129.3 0.7 copy.242
  130.0 7.0 %all-to-all-start.5 = ((bf16[2,64,256]{2,0,1:T(2,128)(2,1)}), bf16[2,64,256]{2,0,1:T(2,128)(2,1)S(1)}, u32[]{:S(2)}, u32[]{:S(2)}) async-start(bf16[2,64,256]{2,0,1:T(2,128)(2,1)} %copy.242), calls=%async_computation.5 | async-start | bytes 131072 | tf_op jit(solution)/shard_map/all_to_all | solution.py:216
  138.3 0.6 convolution_add_fusion.3
  138.9 0.6 convolution_subtract_fusion.3
  139.6 0.9 fusion.26
  140.5 0.9 fusion.4
  141.6 0.7 copy.223
  142.3 6.9 %all-to-all-done.5 = bf16[2,64,256]{2,0,1:T(2,128)(2,1)S(1)} async-done(((bf16[2,64,256]{2,0,1:T(2,128)(2,1)}), bf16[2,64,256]{2,0,1:T(2,128)(2,1)S(1)}, u32[]{:S(2)}, u32[]{:S(2)}) %all-to-all-start.5) | async-done | bytes 65568 | tf_op jit(solution)/shard_map/all_to_all | solution.py:216
  149.2 5.8 %all-to-all-start.2 = ((bf16[2,64,256]{2,0,1:T(2,128)(2,1)}), bf16[2,64,256]{2,0,1:T(2,128)(2,1)S(1)}, u32[]{:S(2)}, u32[]{:S(2)}) async-start(bf16[2,64,256]{2,0,1:T(2,128)(2,1)} %copy.223), calls=%async_computation.2 | async-start | bytes 131072 | tf_op jit(solution)/shard_map/all_to_all | solution.py:209
  156.2 275.6 %all-reduce = (f32[128,64]{0,1:T(8,128)S(1)}, f32[64,33]{0,1:T(8,128)S(1)}) all-reduce(f32[128,64]{0,1:T(8,128)S(1)} %fusion.417, f32[64,33]{0,1:T(8,128)S(1)} %fusion.423), channel_id=1, replica_groups=mesh['ctx'=64,'tp'=8] {'ctx'}, use_global_device_ids=true, to_apply=%region_0.1 | all-reduce | flops 10304 | bytes 82432 | tf_op jit(solution)/shard_map/psum | solution.py:233
  431.8 27.4 %psum.23 = f32[64,33]{0,1:T(8,128)S(1)} all-reduce(f32[64,33]{0,1:T(8,128)S(1)} %get-tuple-element.7), channel_id=1, replica_groups=mesh['ctx'=64,'tp'=8] {'tp'}, use_global_device_ids=true, to_apply=%region_2.3 | all-reduce | flops 2112 | bytes 16896 | tf_op jit(solution)/shard_map/psum | solution.py:12
  459.9 0.7 fusion.30
  460.6 15.5 %collective-permute-start.3 = (bf16[128,6]{1,0:T(8,128)(2,1)S(1)}, bf16[128,6]{1,0:T(8,128)(2,1)S(1)}, u32[]{:S(2)}, u32[]{:S(2)}) collective-permute-start(bf16[128,6]{1,0:T(8,128)(2,1)S(1)} %slice.333), channel_id=1, source_target_pairs={{8,0},{16,8},{24,16},{32,24},{40,32},{48,40},{56,48},{64,56},{72,6... | collective-permute-start | bytes 4616 | tf_op jit(solution)/shard_map/ppermute | solution.py:18
  476.9 1.0 fusion.51
  (100 shorter events, 13.3 us)
Async XLA Ops:
  0.6 8.8 %copy-start = (f32[128,64]{0,1:T(8,128)S(1)}, f32[128,64]{0,1:T(8,128)}, u32[]{:S(2)}) copy-start(f32[128,64]{0,1:T(8,128)} %param.16) | copy-start | bytes 98308
  1.5 32.3 %collective-permute-start = (bf16[128,6]{1,0:T(8,128)(2,1)S(1)}, bf16[128,6]{1,0:T(8,128)(2,1)S(1)}, u32[]{:S(2)}, u32[]{:S(2)}) collective-permute-start(bf16[128,6]{1,0:T(8,128)(2,1)S(1)} %slice.242), channel_id=1, source_target_pairs={{0,8},{8,16},{16,24},{24,32},{32,40},{40,48},{48,56},{56,64},{64,7... | collective-permute-start | bytes 4616 | tf_op jit(solution)/shard_map/ppermute | solution.py:18
  7.5 0.7 copy-start.9
  8.2 0.7 copy-start.5
  8.2 0.7 copy-start.7
  10.4 15.5 %copy-start.3 = (bf16[128,256]{1,0:T(8,128)(2,1)S(1)}, bf16[128,256]{1,0:T(8,128)(2,1)}, u32[]{:S(2)}) copy-start(bf16[128,256]{1,0:T(8,128)(2,1)} %param.12) | copy-start | bytes 196612
  10.4 27.7 %all-to-all-start = ((bf16[64,2,256]{2,1,0:T(2,128)(2,1)}), bf16[64,2,256]{2,1,0:T(2,128)(2,1)S(1)}, u32[]{:S(2)}, u32[]{:S(2)}) async-start(bf16[64,2,256]{2,1,0:T(2,128)(2,1)} %all_to_all.60), calls=%async_computation | async-start | bytes 131072 | tf_op jit(solution)/shard_map/all_to_all | solution.py:204
  25.9 3.6 copy-start.4
  26.0 59.8 %collective-permute-start.2 = (bf16[128,6]{1,0:T(8,128)(2,1)S(1)}, bf16[128,6]{1,0:T(8,128)(2,1)S(1)}, u32[]{:S(2)}, u32[]{:S(2)}) collective-permute-start(bf16[128,6]{1,0:T(8,128)(2,1)S(1)} %slice.274), channel_id=1, source_target_pairs={{0,8},{8,16},{16,24},{24,32},{32,40},{40,48},{48,56},{56,64},{64,7... | collective-permute-start | bytes 4616 | tf_op jit(solution)/shard_map/ppermute | solution.py:18
  29.6 2.7 copy-start.6
  29.6 56.3 %collective-permute-start.1 = (bf16[128,6]{1,0:T(8,128)(2,1)S(1)}, bf16[128,6]{1,0:T(8,128)(2,1)S(1)}, u32[]{:S(2)}, u32[]{:S(2)}) collective-permute-start(bf16[128,6]{1,0:T(8,128)(2,1)S(1)} %slice.258), channel_id=1, source_target_pairs={{0,8},{8,16},{16,24},{24,32},{32,40},{40,48},{48,56},{56,64},{64,7... | collective-permute-start | bytes 4616 | tf_op jit(solution)/shard_map/ppermute | solution.py:18
  33.0 0.9 copy-start.2
  33.1 0.7 copy-start.8
  33.8 0.8 copy-start.1
  38.1 21.5 %all-to-all-start.3 = ((bf16[64,2,256]{2,1,0:T(2,128)(2,1)}), bf16[64,2,256]{2,1,0:T(2,128)(2,1)S(1)}, u32[]{:S(2)}, u32[]{:S(2)}) async-start(bf16[64,2,256]{2,1,0:T(2,128)(2,1)} %all_to_all.67), calls=%async_computation.3 | async-start | bytes 131072 | tf_op jit(solution)/shard_map/all_to_all | solution.py:210
  80.9 17.0 %all-to-all-start.4 = ((bf16[2,64,256]{2,0,1:T(2,128)(2,1)}), bf16[2,64,256]{2,0,1:T(2,128)(2,1)S(1)}, u32[]{:S(2)}, u32[]{:S(2)}) async-start(bf16[2,64,256]{2,0,1:T(2,128)(2,1)} %copy.236), calls=%async_computation.4 | async-start | bytes 131072 | tf_op jit(solution)/shard_map/all_to_all | solution.py:215
  98.5 11.8 %collective-permute-start.5 = (bf16[128,6]{1,0:T(8,128)(2,1)S(1)}, bf16[128,6]{1,0:T(8,128)(2,1)S(1)}, u32[]{:S(2)}, u32[]{:S(2)}) collective-permute-start(bf16[128,6]{1,0:T(8,128)(2,1)S(1)} %slice.349), channel_id=1, source_target_pairs={{8,0},{16,8},{24,16},{32,24},{40,32},{48,40},{56,48},{64,56},{72,6... | collective-permute-start | bytes 4616 | tf_op jit(solution)/shard_map/ppermute | solution.py:18
  101.9 18.2 %all-to-all-start.1 = ((bf16[64,2,256]{2,1,0:T(2,128)(2,1)}), bf16[64,2,256]{2,1,0:T(2,128)(2,1)S(1)}, u32[]{:S(2)}, u32[]{:S(2)}) async-start(bf16[64,2,256]{2,1,0:T(2,128)(2,1)} %all_to_all.63), calls=%async_computation.1 | async-start | bytes 131072 | tf_op jit(solution)/shard_map/all_to_all | solution.py:203
  108.0 5.5 %collective-permute-start.4 = (bf16[128,6]{1,0:T(8,128)(2,1)S(1)}, bf16[128,6]{1,0:T(8,128)(2,1)S(1)}, u32[]{:S(2)}, u32[]{:S(2)}) collective-permute-start(bf16[128,6]{1,0:T(8,128)(2,1)S(1)} %slice.341), channel_id=1, source_target_pairs={{8,0},{16,8},{24,16},{32,24},{40,32},{48,40},{56,48},{64,56},{72,6... | collective-permute-start | bytes 4616 | tf_op jit(solution)/shard_map/ppermute | solution.py:18
  130.0 19.1 %all-to-all-start.5 = ((bf16[2,64,256]{2,0,1:T(2,128)(2,1)}), bf16[2,64,256]{2,0,1:T(2,128)(2,1)S(1)}, u32[]{:S(2)}, u32[]{:S(2)}) async-start(bf16[2,64,256]{2,0,1:T(2,128)(2,1)} %copy.242), calls=%async_computation.5 | async-start | bytes 131072 | tf_op jit(solution)/shard_map/all_to_all | solution.py:216
  149.2 310.6 %all-to-all-start.2 = ((bf16[2,64,256]{2,0,1:T(2,128)(2,1)}), bf16[2,64,256]{2,0,1:T(2,128)(2,1)S(1)}, u32[]{:S(2)}, u32[]{:S(2)}) async-start(bf16[2,64,256]{2,0,1:T(2,128)(2,1)} %copy.223), calls=%async_computation.2 | async-start | bytes 131072 | tf_op jit(solution)/shard_map/all_to_all | solution.py:209
  460.6 16.3 %collective-permute-start.3 = (bf16[128,6]{1,0:T(8,128)(2,1)S(1)}, bf16[128,6]{1,0:T(8,128)(2,1)S(1)}, u32[]{:S(2)}, u32[]{:S(2)}) collective-permute-start(bf16[128,6]{1,0:T(8,128)(2,1)S(1)} %slice.333), channel_id=1, source_target_pairs={{8,0},{16,8},{24,16},{32,24},{40,32},{48,40},{56,48},{64,56},{72,6... | collective-permute-start | bytes 4616 | tf_op jit(solution)/shard_map/ppermute | solution.py:18
